TPU v7x, 32 devices: a whole 2x2x4 slice. The times are simulated.
32 devices in a mesh: groups: 2 (over x), span: 16 (over z, y, core).
Axes of the slice: x: 2, y: 2, z: 4, core: 2. Of those that a mesh axis runs over, the one named last changes fastest.
Arguments:
- queries: bfloat16 [8192, 2560], P(('groups', 'span')), parts along dimension 0, may hold values from -100 to 100
- cross_queries: bfloat16 [8192, 2560], P(('groups', 'span')), parts along dimension 0, may hold values from -100 to 100
- frame_kv: bfloat16 [8192, 5120], P(('groups', 'span')), parts along dimension 0, may hold values from -7 to 7
- sink_kv: bfloat16 [32, 64, 5120], P(('groups', 'span')), parts along dimension 0, may hold values from -5 to 5
- prompt_kv: bfloat16 [4, 512, 5120], P('groups', 'span'), parts along dimension 0, may hold values from -7 to 7
- switch: int32 [8], P('groups'), parts along dimension 0, may hold values from 0 to 4
Outputs:
- self_out: bfloat16 [8192, 2560], P(('groups', 'span')), parts along dimension 0
- cross_out: bfloat16 [8192, 2560], P(('groups', 'span')), parts along dimension 0
There are 2 independent parts, one for each index of `groups`. A program takes and returns all parts, laid end to end along the dimension named above; each array names one. Nothing has to cross between parts.
All inputs are finite; a program needn't handle non-finite values.
Results may differ from a plain program's by a relative error of at most 0.006.
Values may be sent and summed in bfloat16 or wider, within the bound.
A program may use at most 128 MiB of HBM per device.

v0:
```python
import math

import jax
import jax.numpy as jnp
from jax import lax
from jax.sharding import PartitionSpec as P

HEADS = 20
HDIM = 128
WIN = 4


def passed_along(value, axis, steps):
    count = lax.axis_size(axis)
    pairs = [(source, (source + steps) % count) for source in range(count)]
    return lax.ppermute(value, axis, pairs)


def blend_heads(query_rows, key_rows, usable):
    rows_here = query_rows.shape[0]
    key_count = key_rows.shape[0]
    width = HEADS * HDIM
    bundle = 4
    scaling = 1.0 / math.sqrt(HDIM)
    blended_parts = []
    for leading in range(0, HEADS, bundle):
        low = leading * HDIM
        high = (leading + bundle) * HDIM
        query_block = query_rows[:, low:high].reshape(rows_here, bundle, HDIM)
        key_block = key_rows[:, low:high].reshape(key_count, bundle, HDIM)
        value_block = key_rows[:, width + low : width + high].reshape(key_count, bundle, HDIM)
        scores = (
            jnp.einsum("qhd,khd->hqk", query_block, key_block, preferred_element_type=jnp.float32)
            * scaling
        )
        scores = jnp.where(usable[None, None, :], scores, -jnp.inf)
        row_max = jnp.max(scores, axis=-1, keepdims=True)
        weights = jnp.exp(scores - row_max)
        totals = jnp.sum(weights, axis=-1)
        blended = jnp.einsum(
            "hqk,khd->qhd",
            weights.astype(jnp.bfloat16),
            value_block,
            preferred_element_type=jnp.float32,
        )
        blended = blended / jnp.transpose(totals)[:, :, None]
        blended_parts.append(blended.astype(jnp.bfloat16).reshape(rows_here, bundle * HDIM))
    return jnp.concatenate(blended_parts, axis=1)


def shards(queries, cross_queries, frame_kv, sink_kv, prompt_kv, switch):
    stream_count = lax.axis_size("span") // WIN
    device = lax.axis_index("span")
    place = device // stream_count
    stream_of = device % stream_count
    stream_ids = jnp.arange(switch.shape[0], dtype=jnp.int32)
    switch_at = jnp.sum(jnp.where(stream_ids == stream_of, switch, 0))
    prompt_pick = (place >= switch_at).astype(jnp.int32)
    rows_here = queries.shape[0]
    width = HEADS * HDIM
    own_sink = sink_kv.reshape(sink_kv.shape[1], sink_kv.shape[2])
    frame_parts = [frame_kv]
    frame_flags = [jnp.array(True)]
    sink_parts = [own_sink]
    carried_frame = frame_kv
    carried_sink = own_sink
    for offset in range(1, WIN):
        carried_frame, carried_sink = passed_along(
            (carried_frame, carried_sink), "span", stream_count
        )
        frame_parts.append(carried_frame)
        frame_flags.append(place >= offset)
        sink_parts.append(carried_sink)
    sink_rows = jnp.concatenate(sink_parts, axis=0)
    key_rows = jnp.concatenate([sink_rows] + frame_parts, axis=0)
    usable = jnp.concatenate(
        [jnp.ones((sink_rows.shape[0],), jnp.bool_)]
        + [
            jnp.broadcast_to(flag, (piece.shape[0],))
            for piece, flag in zip(frame_parts, frame_flags)
        ]
    )
    self_out = blend_heads(queries, key_rows, usable)
    query_heads = cross_queries.reshape(rows_here, HEADS, HDIM)
    scaling = 1.0 / math.sqrt(HDIM)
    maxima = jnp.full((HEADS, rows_here), -jnp.inf, jnp.float32)
    sums = jnp.zeros((HEADS, rows_here), jnp.float32)
    accum = jnp.zeros((rows_here, HEADS, HDIM), jnp.float32)
    picked = lax.dynamic_index_in_dim(
        lax.all_gather(prompt_kv, "span", axis=1, tiled=True), prompt_pick, 0, keepdims=False
    )
    piece_rows = picked.shape[0]
    key_heads = picked[:, :width].reshape(piece_rows, HEADS, HDIM)
    value_heads = picked[:, width:].reshape(piece_rows, HEADS, HDIM)
    scores = (
        jnp.einsum("qhd,khd->hqk", query_heads, key_heads, preferred_element_type=jnp.float32)
        * scaling
    )
    new_max = jnp.max(scores, axis=-1)
    rescale = jnp.exp(maxima - new_max)
    weights = jnp.exp(scores - new_max[:, :, None])
    sums = sums * rescale + jnp.sum(weights, axis=-1)
    added = jnp.einsum(
        "hqk,khd->qhd",
        weights.astype(jnp.bfloat16),
        value_heads,
        preferred_element_type=jnp.float32,
    )
    accum = accum * jnp.transpose(rescale)[:, :, None] + added
    maxima, sums, accum = (new_max, sums, accum)
    cross_out = (
        (accum / jnp.transpose(sums)[:, :, None]).astype(jnp.bfloat16).reshape(rows_here, width)
    )
    return (self_out, cross_out)


def solution(mesh):
    in_specs = (
        P(("groups", "span"), None),
        P(("groups", "span"), None),
        P(("groups", "span"), None),
        P(("groups", "span"), None, None),
        P("groups", "span", None),
        P("groups"),
    )
    out_specs = (P(("groups", "span"), None), P(("groups", "span"), None))
    return jax.shard_map(shards, mesh=mesh, in_specs=in_specs, out_specs=out_specs, check_vma=False)
```

profile of v0, /device:TPU:24, one launch (start us, length us, event | category | flops | bytes accessed | tf_op | source)
XLA Modules:
  0.0 388.3 jit_solution(17533499278320517781)
XLA Ops:
  7.9 3.0 copy.67
  11.0 120.4 %collective-permute-done.3 = bf16[256,5120]{0,1:T(8,128)(2,1)S(1)} collective-permute-done((bf16[256,5120]{0,1:T(8,128)(2,1)S(1)}, bf16[256,5120]{0,1:T(8,128)(2,1)S(1)}, u32[]{:S(2)}, u32[]{:S(2)}) %collective-permute-start.3) | collective-permute-done | bytes 2621472 | tf_op jit(solution)/shard_map/ppermute | solution.py:16
  133.0 56.8 %collective-permute-done.4 = bf16[256,5120]{0,1:T(8,128)(2,1)} collective-permute-done((bf16[256,5120]{0,1:T(8,128)(2,1)S(1)}, bf16[256,5120]{0,1:T(8,128)(2,1)}, u32[]{:S(2)}, u32[]{:S(2)}) %collective-permute-start.4) | collective-permute-done | bytes 2621472 | tf_op jit(solution)/shard_map/ppermute | solution.py:16
  189.8 1.7 collective-permute-start.5
  191.6 68.1 %collective-permute-done = bf16[64,5120]{1,0:T(8,128)(2,1)S(1)} collective-permute-done((bf16[64,5120]{1,0:T(8,128)(2,1)S(1)}, bf16[64,5120]{1,0:T(8,128)(2,1)S(1)}, u32[]{:S(2)}, u32[]{:S(2)}) %collective-permute-start) | collective-permute-done | bytes 655392 | tf_op jit(solution)/shard_map/ppermute | solution.py:16
  260.6 3.7 collective-permute-start.1
  264.3 10.3 %collective-permute-done.1 = bf16[64,5120]{1,0:T(8,128)(2,1)} collective-permute-done((bf16[64,5120]{1,0:T(8,128)(2,1)S(1)}, bf16[64,5120]{1,0:T(8,128)(2,1)}, u32[]{:S(2)}, u32[]{:S(2)}) %collective-permute-start.1) | collective-permute-done | bytes 655392 | tf_op jit(solution)/shard_map/ppermute | solution.py:16
  274.6 4.4 %collective-permute-start.2 = (bf16[64,5120]{1,0:T(8,128)(2,1)}, bf16[64,5120]{1,0:T(8,128)(2,1)}, u32[]{:S(2)}, u32[]{:S(2)}) collective-permute-start(bf16[64,5120]{1,0:T(8,128)(2,1)} %collective-permute-done.1), channel_id=1, source_target_pairs={{0,4},{1,5},{2,6},{3,7},{4,8},{5,9},{6,10},{7,11},{8,12},{9,13},{1... | collective-permute-start | bytes 1966088 | tf_op jit(solution)/shard_map/ppermute | solution.py:16
  281.6 2.2 fusion.90
  283.8 1.8 copy.119
  287.8 2.4 copy.94
  290.3 2.3 copy.64
  292.6 2.3 copy.65
  295.0 2.3 copy.66
  297.3 20.5 %concatenate.12 = bf16[1280,5120]{0,1:T(8,128)(2,1)} concatenate(bf16[64,5120]{0,1:T(8,128)(2,1)} %bitcast.186, bf16[64,5120]{0,1:T(8,128)(2,1)} %copy.64, bf16[64,5120]{0,1:T(8,128)(2,1)} %copy.65, bf16[64,5120]{0,1:T(8,128)(2,1)} %copy.66, bf16[256,5120]{0,1:T(8,128)(2,1)S(1)} %copy.67, bf16[256,5120]{0,1:T(8,128)(2,1)} %copy-done.3, bf16[256,5120]{0,1:T(8,128)(2,1)} %collective-permute-done.4, ...), dimensions={0} | concatenate | bytes 26214400 | tf_op jit(solution)/shard_map/concatenate | solution.py:75
  317.8 8.1 %fusion.88 = (bf16[1280,512]{0,1:T(8,128)(2,1)S(1)}, bf16[1280,512]{0,1:T(8,128)(2,1)S(1)}, bf16[1280,512]{0,1:T(8,128)(2,1)}, bf16[1280,512]{0,1:T(8,128)(2,1)}...) fusion(bf16[1280,5120]{0,1:T(8,128)(2,1)} %concatenate.12), kind=kLoop, calls=%fused_computation.78 | loop fusion | bytes 26214400 | tf_op jit(solution)/shard_map/slice | solution.py:30
  325.9 1.8 bitcast_reduce_fusion.5
  328.5 1.7 fusion.83
  330.2 1.8 copy.88
  332.0 2.6 bitcast_reduce_fusion.4
  335.9 1.7 fusion.77
  337.6 1.8 copy.89
  339.4 2.6 bitcast_reduce_fusion.3
  343.3 1.7 fusion.71
  346.2 2.6 bitcast_reduce_fusion.2
  352.9 1.9 bitcast_reduce_fusion.1
  360.3 2.8 dynamic-slice_bitcast_fusion
  363.1 1.9 fusion.89
  365.0 4.4 %copy.97 = bf16[512,2560]{0,1:T(8,128)(2,1)} copy(bf16[512,2560]{1,0:T(8,128)(2,1)} %get-tuple-element.19) | data formatting | bytes 5242880 | tf_op jit(solution)/shard_map/slice | solution.py:94
  369.4 2.6 copy.93
  372.1 3.7 bitcast_reduce_fusion
  377.6 2.3 fusion.33
  (60 shorter events, 24.9 us)
Async XLA Ops:
  7.2 353.1 %all-gather.2.cloned.1.call-start = ((), (), s32[]{:S(2)}) async-start(), calls=%async_computation | async-start | bytes 11141120 | tf_op jit(solution)/shard_map/all_gather | solution.py:90
  7.9 183.6 %copy-start.8 = (bf16[1,64,5120]{2,1,0:T(8,128)(2,1)S(1)}, bf16[1,64,5120]{2,1,0:T(8,128)(2,1)}, u32[]{:S(2)}) copy-start(bf16[1,64,5120]{2,1,0:T(8,128)(2,1)} %param.9) | copy-start | bytes 1966084
  7.9 272.5 %copy-start.10 = (s32[4]{0:T(128)S(1)}, s32[4]{0:T(128)}, u32[]{:S(2)}) copy-start(s32[4]{0:T(128)} %param.11) | copy-start | bytes 52
  11.0 120.5 %collective-permute-start.3 = (bf16[256,5120]{0,1:T(8,128)(2,1)S(1)}, bf16[256,5120]{0,1:T(8,128)(2,1)S(1)}, u32[]{:S(2)}, u32[]{:S(2)}) collective-permute-start(bf16[256,5120]{0,1:T(8,128)(2,1)S(1)} %copy.67), channel_id=1, source_target_pairs={{0,4},{1,5},{2,6},{3,7},{4,8},{5,9},{6,10},{7,11},{8,12},{9,13},{1... | collective-permute-start | bytes 7864328 | tf_op jit(solution)/shard_map/ppermute | solution.py:16
  131.4 1.5 copy-start.3
  133.0 56.8 %collective-permute-start.4 = (bf16[256,5120]{0,1:T(8,128)(2,1)S(1)}, bf16[256,5120]{0,1:T(8,128)(2,1)}, u32[]{:S(2)}, u32[]{:S(2)}) collective-permute-start(bf16[256,5120]{0,1:T(8,128)(2,1)S(1)} %collective-permute-done.3), channel_id=1, source_target_pairs={{0,4},{1,5},{2,6},{3,7},{4,8},{5,9},{6,10},{7,11},{8,12},{9,13},{1... | collective-permute-start | bytes 7864328 | tf_op jit(solution)/shard_map/ppermute | solution.py:16
  189.8 107.5 %collective-permute-start.5 = (bf16[256,5120]{0,1:T(8,128)(2,1)}, bf16[256,5120]{0,1:T(8,128)(2,1)}, u32[]{:S(2)}, u32[]{:S(2)}) collective-permute-start(bf16[256,5120]{0,1:T(8,128)(2,1)} %collective-permute-done.4), channel_id=1, source_target_pairs={{0,4},{1,5},{2,6},{3,7},{4,8},{5,9},{6,10},{7,11},{8,12},{9,13},{1... | collective-permute-start | bytes 7864328 | tf_op jit(solution)/shard_map/ppermute | solution.py:16
  191.5 68.1 %collective-permute-start = (bf16[64,5120]{1,0:T(8,128)(2,1)S(1)}, bf16[64,5120]{1,0:T(8,128)(2,1)S(1)}, u32[]{:S(2)}, u32[]{:S(2)}) collective-permute-start(bf16[64,5120]{1,0:T(8,128)(2,1)S(1)} %bitcast.210), channel_id=1, source_target_pairs={{0,4},{1,5},{2,6},{3,7},{4,8},{5,9},{6,10},{7,11},{8,12},{9,13},{1... | collective-permute-start | bytes 1966088 | tf_op jit(solution)/shard_map/ppermute | solution.py:16
  259.7 0.9 copy-start.9
  260.6 14.0 %collective-permute-start.1 = (bf16[64,5120]{1,0:T(8,128)(2,1)S(1)}, bf16[64,5120]{1,0:T(8,128)(2,1)}, u32[]{:S(2)}, u32[]{:S(2)}) collective-permute-start(bf16[64,5120]{1,0:T(8,128)(2,1)S(1)} %collective-permute-done), channel_id=1, source_target_pairs={{0,4},{1,5},{2,6},{3,7},{4,8},{5,9},{6,10},{7,11},{8,12},{9,13},{1... | collective-permute-start | bytes 1966088 | tf_op jit(solution)/shard_map/ppermute | solution.py:16
  274.6 20.4 %collective-permute-start.2 = (bf16[64,5120]{1,0:T(8,128)(2,1)}, bf16[64,5120]{1,0:T(8,128)(2,1)}, u32[]{:S(2)}, u32[]{:S(2)}) collective-permute-start(bf16[64,5120]{1,0:T(8,128)(2,1)} %collective-permute-done.1), channel_id=1, source_target_pairs={{0,4},{1,5},{2,6},{3,7},{4,8},{5,9},{6,10},{7,11},{8,12},{9,13},{1... | collective-permute-start | bytes 1966088 | tf_op jit(solution)/shard_map/ppermute | solution.py:16
  317.8 8.2 %copy-start.5 = (bf16[256,512]{0,1:T(8,128)(2,1)S(1)}, bf16[256,512]{0,1:T(8,128)(2,1)}, u32[]{:S(2)}) copy-start(bf16[256,512]{0,1:T(8,128)(2,1)} %copy.119) | copy-start | bytes 786436
  334.6 1.3 copy-start.2
  342.0 1.3 copy-start.1
  348.7 1.3 copy-start
  355.4 1.2 copy-start.6
  355.4 1.9 copy-start.7
  375.8 1.8 copy-start.4
Sparse Core Ops, SparseCore 0:
  10.3 125.3 all-gather.1
where the time goes:
time: 391 us; the launch traced here: 388 us
  waiting for transfers between devices  256 us (65%)
  local copies, waits for them, and re-layouts  75.8 us (19%)
  matrix products  25.3 us (6%)
  between operations  15 us (4%)
  starting transfers between devices  9.94 us (3%)
  other arithmetic  5.91 us (2%)
    ppermute x6, waiting for transfers between devices, passed_along(): return lax.ppermute(value, axis, pairs)  256 us
    concatenate x1, local copies, waits for them, and re-layouts, shards(): key_rows = jnp.concatenate([sink_rows] + frame_parts, axis=0)  20.5 us
    unnamed x35, local copies, waits for them, and re-layouts  19.6 us
    dot_general x5, matrix products, blend_heads(): jnp.einsum('qhd,khd->hqk', query_block, key_block, preferred_element_type...  11.4 us
    ppermute x6, starting transfers between devices, passed_along(): return lax.ppermute(value, axis, pairs)  9.91 us
    slice x1, local copies, waits for them, and re-layouts, blend_heads(): key_block = key_rows[:, low:high].reshape(key_count, bundle, HDIM)  8.14 us
    dot_general x5, matrix products, blend_heads(): jnp.einsum('hqk,khd->qhd', weights.astype(jnp.bfloat16), value_block, pre...  7.99 us
  transfers between devices with their start and end apart: 7, of which 4 were waited for; matrix products, arithmetic and copies ran while one was open for 21% of the time, Pallas kernels for 0%

commit v1 on v0

v1 whole, which is shorter than its diff:
```python
import functools
import math

import jax
import jax.numpy as jnp
from jax import lax
from jax.experimental import pallas as pl
from jax.experimental.pallas import tpu as pltpu
from jax.sharding import PartitionSpec as P

HEADS = 20
HDIM = 128
WIN = 4
BUNDLE = 4
CHUNKS = HEADS // BUNDLE
BW = BUNDLE * HDIM
WIDTH = HEADS * HDIM
SCALE = 1.0 / math.sqrt(HDIM)
LOG2E = 1.4426950408889634
MESH = pl.DeviceIdType.MESH


def attend(query, pieces):
    scores = [
        lax.dot_general(query, keys, (((1,), (1,)), ((), ())), preferred_element_type=jnp.float32)
        for keys, _ in pieces
    ]
    peak = functools.reduce(
        jnp.maximum, [jnp.max(piece, axis=1, keepdims=True) for piece in scores]
    )
    total, blended = None, None
    for piece, (_, values) in zip(scores, pieces):
        weights = jnp.exp2((piece - peak) * (SCALE * LOG2E))
        part_sum = jnp.sum(weights, axis=1, keepdims=True)
        part = jnp.dot(weights.astype(jnp.bfloat16), values, preferred_element_type=jnp.float32)
        total = part_sum if total is None else total + part_sum
        blended = part if blended is None else blended + part
    return blended / total, peak * (SCALE * LOG2E), total


def cols(chunk, width=BW, base=0):
    return pl.ds(pl.multiple_of(base + chunk * width, 128), width)


def head_cols(head, base=0):
    return pl.ds(pl.multiple_of(base + head * HDIM, 128), HDIM)


def self_kernel(
    q_ref, kv_ref, sink_ref, out_ref,
    kv_prev, sinks, q_in, o_send, o_recv, st_send, st_recv,
    kv_s, kv_r, q_s, q_r, s_s, s_r, o_s, o_r, st_s, st_r,
):
    stride = lax.axis_size("span") // WIN
    me = lax.axis_index("span")
    place = me // stride
    stream = me % stride
    rows_s = sink_ref.shape[0]

    def at_place(index):
        return {"span": index * stride + stream}

    def remote(src, dst, send, recv, index):
        return pltpu.make_async_remote_copy(
            src_ref=src, dst_ref=dst, send_sem=send, recv_sem=recv,
            device_id=at_place(index), device_id_type=MESH,
        )

    def kv_copies(chunk):
        pairs = []
        for part in range(2):
            where = cols(chunk, BW, part * WIDTH)
            pairs.append((kv_ref.at[:, where], kv_prev.at[:, where]))
        for part in range(2):
            where = cols(chunk, BW, part * WIDTH)
            pairs.append((sink_ref.at[:, where], sinks.at[0:rows_s, where]))
        return [
            remote(src, dst, kv_s.at[i, chunk], kv_r.at[i, chunk], 1)
            for i, (src, dst) in enumerate(pairs)
        ]

    def q_copy(chunk, slot, index):
        return remote(
            q_ref.at[:, cols(chunk)], q_in.at[slot, :, cols(chunk)],
            q_s.at[slot, chunk], q_r.at[slot, chunk], index,
        )

    def sink_copy(which, index, own):
        where = pl.ds(which * rows_s, rows_s)
        src = sink_ref if own else sinks.at[where, :]
        return remote(src, sinks.at[where, :], s_s.at[which], s_r.at[which], index)

    def o_copy(chunk, slot, index):
        return remote(
            o_send.at[slot, :, cols(chunk)], o_recv.at[slot, :, cols(chunk)],
            o_s.at[slot, chunk], o_r.at[slot, chunk], index,
        )

    def st_copy(slot, index):
        return remote(st_send.at[slot], st_recv.at[slot], st_s.at[slot], st_r.at[slot], index)

    lanes = lax.broadcasted_iota(jnp.int32, st_send.shape[1:], 1)

    def partial(slot, chunk, pieces_of):
        stats = st_send[slot]
        for inner in range(BUNDLE):
            head = chunk * BUNDLE + inner
            blended, peak, total = attend(q_in[slot, :, head_cols(head)], pieces_of(head))
            o_send[slot, :, head_cols(head)] = blended.astype(jnp.bfloat16)
            stats = jnp.where(lanes == head, peak + jnp.log2(total), stats)
        st_send[slot] = stats

    def final(pieces_of, slots):
        def step(chunk, carry):
            for inner in range(BUNDLE):
                head = chunk * BUNDLE + inner
                where = head_cols(head)
                blended, peak, total = attend(q_ref[:, where], pieces_of(head))
                if slots:
                    levels = [peak + jnp.log2(total)]
                    outs = [blended]
                    for slot in slots:
                        levels.append(
                            jnp.sum(jnp.where(lanes == head, st_recv[slot], 0.0), axis=1, keepdims=True)
                        )
                        outs.append(o_recv[slot, :, where].astype(jnp.float32))
                    top = functools.reduce(jnp.maximum, levels)
                    shares = [jnp.exp2(level - top) for level in levels]
                    whole = functools.reduce(jnp.add, shares)
                    blended = functools.reduce(
                        jnp.add, [out * share for out, share in zip(outs, shares)]
                    ) / whole
                out_ref[:, where] = blended.astype(jnp.bfloat16)
            return carry
        lax.fori_loop(0, CHUNKS, step, 0)

    def pair(ref, head, low=None, high=None):
        rows = slice(low, high)
        return ref[rows, head_cols(head)], ref[rows, head_cols(head, WIDTH)]

    barrier = pltpu.get_barrier_semaphore()
    for step in range(1, WIN):
        pl.semaphore_signal(
            barrier, inc=1, device_id=at_place((place + step) % WIN), device_id_type=MESH
        )
    pl.semaphore_wait(barrier, WIN - 1)

    @pl.when(place == 0)
    def _():
        def send(chunk, carry):
            for copy in kv_copies(chunk):
                copy.start()
            return carry
        lax.fori_loop(0, CHUNKS, send, 0)
        sinks[0:rows_s, :] = sink_ref[...]
        for which in (1, 2, 3):
            sink_copy(which, 0, False).wait_recv()
        final(lambda head: [pair(sinks, head), pair(kv_ref, head)], ())

        def drain(chunk, carry):
            for copy in kv_copies(chunk):
                copy.wait_send()
            return carry
        lax.fori_loop(0, CHUNKS, drain, 0)

    @pl.when(place == 1)
    def _():
        sink_copy(1, 0, True).start()
        sinks[rows_s : 2 * rows_s, :] = sink_ref[...]
        st_send[...] = jnp.zeros_like(st_send)

        def work(chunk, carry):
            for copy in kv_copies(chunk):
                copy.wait_recv()
            for slot in range(2):
                q_copy(chunk, slot, 1).wait_recv()
                partial(
                    slot, chunk,
                    lambda head: [
                        pair(sinks, head, 0, 2 * rows_s), pair(kv_prev, head), pair(kv_ref, head)
                    ],
                )
                o_copy(chunk, slot, 2 + slot).start()
            return carry
        lax.fori_loop(0, CHUNKS - 2, work, 0)
        sink_copy(2, 1, False).wait_recv()
        sink_copy(2, 0, False).start()
        lax.fori_loop(CHUNKS - 2, CHUNKS - 1, work, 0)
        sink_copy(3, 1, False).wait_recv()
        sink_copy(3, 0, False).start()
        lax.fori_loop(CHUNKS - 1, CHUNKS, work, 0)
        for slot in range(2):
            st_copy(slot, 2 + slot).start()
        final(lambda head: [pair(sinks, head), pair(kv_prev, head), pair(kv_ref, head)], ())
        for which in (1, 2, 3):
            sink_copy(which, 0, which == 1).wait_send()

        def drain(chunk, carry):
            for slot in range(2):
                o_copy(chunk, slot, 2 + slot).wait_send()
            return carry
        lax.fori_loop(0, CHUNKS, drain, 0)
        for slot in range(2):
            st_copy(slot, 2 + slot).wait_send()

    @pl.when(place == 2)
    def _():
        for chunk in range(CHUNKS):
            if chunk == 2:
                sink_copy(2, 1, True).start()
            q_copy(chunk, 0, 1).start()
        sinks[2 * rows_s : 3 * rows_s, :] = sink_ref[...]
        st_send[0] = jnp.zeros_like(st_send[0])
        sink_copy(3, 2, False).wait_recv()
        sink_copy(3, 1, False).start()

        def work(chunk, carry):
            q_copy(chunk, 0, 2).wait_recv()
            partial(
                0, chunk,
                lambda head: [pair(sinks, head, 2 * rows_s, 3 * rows_s), pair(kv_ref, head)],
            )
            o_copy(chunk, 0, 3).start()
            return carry
        lax.fori_loop(0, CHUNKS, work, 0)
        st_copy(0, 3).start()

        def arrive(chunk, carry):
            o_copy(chunk, 0, 2).wait_recv()
            return carry
        lax.fori_loop(0, CHUNKS, arrive, 0)
        st_copy(0, 2).wait_recv()
        final(lambda head: [pair(sinks, head, 2 * rows_s, 4 * rows_s), pair(kv_ref, head)], (0,))
        sink_copy(2, 1, True).wait_send()
        sink_copy(3, 1, False).wait_send()

        def drain(chunk, carry):
            q_copy(chunk, 0, 1).wait_send()
            o_copy(chunk, 0, 3).wait_send()
            return carry
        lax.fori_loop(0, CHUNKS, drain, 0)
        st_copy(0, 3).wait_send()

    @pl.when(place == 3)
    def _():
        for chunk in range(CHUNKS):
            if chunk == 2:
                sink_copy(3, 2, True).start()
            q_copy(chunk, 1, 1).start()
        for chunk in range(CHUNKS):
            q_copy(chunk, 0, 2).start()

        def arrive(chunk, carry):
            for slot in range(2):
                o_copy(chunk, slot, 3).wait_recv()
            return carry
        lax.fori_loop(0, CHUNKS, arrive, 0)
        for slot in range(2):
            st_copy(slot, 3).wait_recv()
        final(lambda head: [pair(sink_ref, head), pair(kv_ref, head)], (0, 1))
        sink_copy(3, 2, True).wait_send()

        def drain(chunk, carry):
            q_copy(chunk, 1, 1).wait_send()
            q_copy(chunk, 0, 2).wait_send()
            return carry
        lax.fori_loop(0, CHUNKS, drain, 0)


def self_attention(queries, frame_kv, own_sink):
    rows = queries.shape[0]
    vmem = pl.BlockSpec(memory_space=pltpu.VMEM)
    dma = pltpu.SemaphoreType.DMA
    return pl.pallas_call(
        self_kernel,
        out_shape=jax.ShapeDtypeStruct((rows, WIDTH), jnp.bfloat16),
        in_specs=[vmem] * 3,
        out_specs=vmem,
        scratch_shapes=[
            pltpu.VMEM((rows, 2 * WIDTH), jnp.bfloat16),
            pltpu.VMEM((WIN * own_sink.shape[0], 2 * WIDTH), jnp.bfloat16),
            pltpu.VMEM((2, rows, WIDTH), jnp.bfloat16),
            pltpu.VMEM((2, rows, WIDTH), jnp.bfloat16),
            pltpu.VMEM((2, rows, WIDTH), jnp.bfloat16),
            pltpu.VMEM((2, rows, 128), jnp.float32),
            pltpu.VMEM((2, rows, 128), jnp.float32),
            dma((4, CHUNKS)), dma((4, CHUNKS)),
            dma((2, CHUNKS)), dma((2, CHUNKS)),
            dma((WIN,)), dma((WIN,)),
            dma((2, CHUNKS)), dma((2, CHUNKS)),
            dma((2,)), dma((2,)),
        ],
        compiler_params=pltpu.CompilerParams(
            collective_id=0, has_side_effects=True, vmem_limit_bytes=56 * 1024 * 1024
        ),
    )(queries, frame_kv, own_sink)


def cross_kernel(pick_ref, q_ref, k_ref, v_ref, out_ref):
    for inner in range(BUNDLE):
        where = slice(inner * HDIM, (inner + 1) * HDIM)
        blended, _, _ = attend(q_ref[:, where], [(k_ref[0, :, where], v_ref[0, :, where])])
        out_ref[:, where] = blended.astype(jnp.bfloat16)


def cross_attention(cross_queries, prompts, pick):
    rows = cross_queries.shape[0]
    tokens = prompts.shape[1]
    return pl.pallas_call(
        cross_kernel,
        out_shape=jax.ShapeDtypeStruct((rows, WIDTH), jnp.bfloat16),
        grid_spec=pltpu.PrefetchScalarGridSpec(
            num_scalar_prefetch=1,
            grid=(CHUNKS,),
            in_specs=[
                pl.BlockSpec((rows, BW), lambda c, pick: (0, c)),
                pl.BlockSpec((1, tokens, BW), lambda c, pick: (pick[0], 0, c)),
                pl.BlockSpec((1, tokens, BW), lambda c, pick: (pick[0], 0, CHUNKS + c)),
            ],
            out_specs=pl.BlockSpec((rows, BW), lambda c, pick: (0, c)),
        ),
    )(pick.reshape(1), cross_queries, prompts, prompts)


def shards(queries, cross_queries, frame_kv, sink_kv, prompt_kv, switch):
    stream_count = lax.axis_size("span") // WIN
    device = lax.axis_index("span")
    place = device // stream_count
    stream_of = device % stream_count
    stream_ids = jnp.arange(switch.shape[0], dtype=jnp.int32)
    switch_at = jnp.sum(jnp.where(stream_ids == stream_of, switch, 0))
    pick = (place >= switch_at).astype(jnp.int32)
    prompts = lax.all_gather(prompt_kv, "span", axis=1, tiled=True)
    own_sink = sink_kv.reshape(sink_kv.shape[1], sink_kv.shape[2])
    self_out = self_attention(queries, frame_kv, own_sink)
    cross_out = cross_attention(cross_queries, prompts, pick)
    return (self_out, cross_out)


def solution(mesh):
    in_specs = (
        P(("groups", "span"), None),
        P(("groups", "span"), None),
        P(("groups", "span"), None),
        P(("groups", "span"), None, None),
        P("groups", "span", None),
        P("groups"),
    )
    out_specs = (P(("groups", "span"), None), P(("groups", "span"), None))
    return jax.shard_map(shards, mesh=mesh, in_specs=in_specs, out_specs=out_specs, check_vma=False)
```

time: 391 us -> 209 us (0.53)
  waiting for transfers between devices: 256 us -> 0.7 us
  Pallas kernels: 0 us -> 191 us
  local copies, waits for them, and re-layouts: 75.8 us -> 1.06 us
  matrix products: 25.3 us -> 0 us
  starting transfers between devices: 9.94 us -> 0.04 us
  other arithmetic: 5.91 us -> 1.29 us
    ppermute x6 -> x0, waiting for transfers between devices: 256 us -> none  [passed_along(): return lax.ppermute(value, axis, pairs)]
    pallas_call x0 -> x2, Pallas kernels: none -> 191 us  [the longest x1 182 us: self_attention(): pl.pallas_call(self_kernel, out_shape=jax.ShapeDtypeStruct((rows, WIDTH),...]
    dot_general x12 -> x0, matrix products: 25.3 us -> none  [the longest x5 11.4 us: blend_heads(): jnp.einsum('qhd,khd->hqk', query_block, key_block, preferred_element_type...]
    concatenate x3 -> x0, local copies, waits for them, and re-layouts: 21.2 us -> none  [the longest x1 20.5 us: shards(): key_rows = jnp.concatenate([sink_rows] + frame_parts, axis=0)]
    slice x5 -> x0, local copies, waits for them, and re-layouts: 19.3 us -> none  [the longest x1 8.14 us: blend_heads(): key_block = key_rows[:, low:high].reshape(key_count, bundle, HDIM)]
    unnamed x35 -> x3, local copies, waits for them, and re-layouts: 19.6 us -> 1.06 us
    ppermute x6 -> x0, starting transfers between devices: 9.91 us -> none  [passed_along(): return lax.ppermute(value, axis, pairs)]
    ppermute x3 -> x0, local copies, waits for them, and re-layouts: 6.97 us -> none  [passed_along(): return lax.ppermute(value, axis, pairs)]
  transfers between devices with their start and end apart: 7 -> 1, of which waited for: 4 -> 0; matrix products, arithmetic and copies ran while one was open for 21% -> 1% of each run, Pallas kernels for 0% -> 87%
where the time goes in v1:
time: 209 us
  Pallas kernels  191 us (91%)
  between operations  14.7 us (7%)
    pallas_call x1, Pallas kernels, self_attention(): pl.pallas_call(self_kernel, out_shape=jax.ShapeDtypeStruct((rows, WIDTH),...  182 us
    pallas_call x1, Pallas kernels, cross_attention(): pl.pallas_call(cross_kernel, out_shape=jax.ShapeDtypeStruct((rows, WIDTH)...  9.08 us
  transfers between devices with their start and end apart: 1, of which 0 were waited for; matrix products, arithmetic and copies ran while one was open for 1% of the time, Pallas kernels for 87%

profile of v1, /device:TPU:24, one launch (start us, length us, event | category | flops | bytes accessed | tf_op | source)
XLA Modules:
  0.0 209.2 jit_solution(10306094658509845341)
XLA Ops:
  7.2 0.0 all-gather.2.cloned.1.call-start
  7.2 0.7 all-gather.2.cloned.1.call-update
  7.9 1.3 fusion
  9.9 182.3 %shard_map.77 = bf16[256,2560]{1,0:T(8,128)(2,1)} custom-call(bf16[256,2560]{1,0:T(8,128)(2,1)} %q_ref.2, bf16[256,5120]{1,0:T(8,128)(2,1)} %kv_ref.1, bf16[64,5120]{1,0:T(8,128)(2,1)} %bitcast.2), custom_call_target="tpu_custom_call" | custom-call | tf_op jit(solution)/shard_map/pallas_call | solution.py:274
  192.2 0.0 all-gather.2.cloned.1.call-done.k_ref.v_ref
  192.2 0.0 copy-start
  192.2 9.1 %shard_map.78 = bf16[256,2560]{1,0:T(8,128)(2,1)} custom-call(s32[1]{0:T(128)} %bitcast.1.pick_ref, bf16[256,2560]{1,0:T(8,128)(2,1)} %q_ref.3, bf16[2,512,5120]{2,1,0:T(8,128)(2,1)} %all-gather.2.cloned.1.call-done.k_ref.v_ref, bf16[2,512,5120]{2,1,0:T(8,128)(2,1)} %all-gather.2.cloned.1.call-done.k_ref.v_ref), custom_call_target="tpu_custom_call" | custom-call | tf_op jit(solution)/shard_map/pallas_call | solution.py:309
  201.3 0.0 copy-done
  201.3 1.1 copy.9
Async XLA Ops:
  7.2 185.0 %all-gather.2.cloned.1.call-start = ((), (), s32[]{:S(2)}) async-start(), calls=%async_computation | async-start | bytes 11141120 | tf_op jit(solution)/shard_map/all_gather | solution.py:333
  192.2 9.1 %copy-start = (bf16[256,2560]{1,0:T(8,128)(2,1)S(1)}, bf16[256,2560]{1,0:T(8,128)(2,1)}, u32[]{:S(2)}) copy-start(bf16[256,2560]{1,0:T(8,128)(2,1)} %shard_map.77) | copy-start | bytes 3932164
Sparse Core Ops, SparseCore 0:
  10.3 135.9 all-gather.1

commit v2 on v1

v2 whole, which is shorter than its diff:
```python
import functools
import math

import jax
import jax.numpy as jnp
from jax import lax
from jax.experimental import pallas as pl
from jax.experimental.pallas import tpu as pltpu
from jax.sharding import PartitionSpec as P

HEADS = 20
HDIM = 128
WIN = 4
BUNDLE = 4
CHUNKS = HEADS // BUNDLE
BW = BUNDLE * HDIM
WIDTH = HEADS * HDIM
SCALE = 1.0 / math.sqrt(HDIM)
LOG2E = 1.4426950408889634
MESH = pl.DeviceIdType.MESH


def attend(query, pieces):
    scores = [
        lax.dot_general(query, keys, (((1,), (1,)), ((), ())), preferred_element_type=jnp.float32)
        for keys, _ in pieces
    ]
    peak = functools.reduce(
        jnp.maximum, [jnp.max(piece, axis=1, keepdims=True) for piece in scores]
    )
    total, blended = None, None
    for piece, (_, values) in zip(scores, pieces):
        weights = jnp.exp2((piece - peak) * (SCALE * LOG2E))
        part_sum = jnp.sum(weights, axis=1, keepdims=True)
        part = jnp.dot(weights.astype(jnp.bfloat16), values, preferred_element_type=jnp.float32)
        total = part_sum if total is None else total + part_sum
        blended = part if blended is None else blended + part
    return blended / total, peak * (SCALE * LOG2E), total


def cols(chunk, width=BW, base=0):
    return pl.ds(pl.multiple_of(base + chunk * width, 128), width)


def head_cols(head, base=0):
    return pl.ds(pl.multiple_of(base + head * HDIM, 128), HDIM)


def self_kernel(with_prompts, *refs):
    if with_prompts:
        (q_ref, kv_ref, sink_ref, prompt_ref, cq_ref, pick_ref, out_ref, cross_ref, *refs) = refs
        (bank, pr_s, pr_r, own_sem, *refs) = refs
    else:
        (q_ref, kv_ref, sink_ref, out_ref, *refs) = refs
    (kv_prev, sinks, q_in, o_send, o_recv, st_send, st_recv,
     kv_s, kv_r, q_s, q_r, s_s, s_r, o_s, o_r, st_s, st_r) = refs
    stride = lax.axis_size("span") // WIN
    me = lax.axis_index("span")
    place = me // stride
    stream = me % stride
    across = (stream + 2) % 4
    beside = stream + 1 - 2 * (stream % 2)
    rows_s = sink_ref.shape[0]
    rows = q_ref.shape[0]

    def at_place(index):
        return {"span": index * stride + stream}

    def remote(src, dst, send, recv, index, line=None):
        return pltpu.make_async_remote_copy(
            src_ref=src, dst_ref=dst, send_sem=send, recv_sem=recv,
            device_id=at_place(index) if line is None else {"span": index * stride + line},
            device_id_type=MESH,
        )

    def kv_copies(chunk):
        pairs = []
        for part in range(2):
            where = cols(chunk, BW, part * WIDTH)
            pairs.append((sink_ref.at[:, where], sinks.at[0:rows_s, where]))
        for part in range(2):
            where = cols(chunk, BW, part * WIDTH)
            pairs.append((kv_ref.at[:, where], kv_prev.at[:, where]))
        return [
            remote(src, dst, kv_s.at[i, chunk], kv_r.at[i, chunk], 1)
            for i, (src, dst) in enumerate(pairs)
        ]

    def q_copy(chunk, slot, index):
        return remote(
            q_ref.at[:, cols(chunk)], q_in.at[slot, :, cols(chunk)],
            q_s.at[slot, chunk], q_r.at[slot, chunk], index,
        )

    def sink_copy(which, index, own):
        where = pl.ds(which * rows_s, rows_s)
        src = sink_ref if own else sinks.at[where, :]
        return remote(src, sinks.at[where, :], s_s.at[which], s_r.at[which], index)

    def o_copy(chunk, slot, index):
        return remote(
            o_send.at[slot, :, cols(chunk)], o_recv.at[slot, :, cols(chunk)],
            o_s.at[slot, chunk], o_r.at[slot, chunk], index,
        )

    def st_copy(chunk, slot, index):
        return remote(
            st_send.at[slot, chunk], st_recv.at[slot, chunk],
            st_s.at[slot, chunk], st_r.at[slot, chunk], index,
        )

    def partial(slot, chunk, pieces_of, index):
        lanes = lax.broadcasted_iota(jnp.int32, (rows, 128), 1)
        stats = jnp.zeros((rows, 128), jnp.float32)
        for inner in range(BUNDLE):
            head = chunk * BUNDLE + inner
            blended, peak, total = attend(q_in[slot, :, head_cols(head)], pieces_of(head))
            o_send[slot, :, head_cols(head)] = blended.astype(jnp.bfloat16)
            stats = jnp.where(lanes == inner, peak + jnp.log2(total), stats)
        st_send[slot, chunk] = jnp.transpose(stats)[0:8]
        o_copy(chunk, slot, index).start()
        st_copy(chunk, slot, index).start()

    def drain_partial(slot, index):
        def drain(chunk, carry):
            o_copy(chunk, slot, index).wait_send()
            st_copy(chunk, slot, index).wait_send()
            return carry
        lax.fori_loop(0, CHUNKS, drain, 0)

    def final(chunk, pieces_of, slots, index):
        levels_in = []
        for slot in slots:
            o_copy(chunk, slot, index).wait_recv()
            st_copy(chunk, slot, index).wait_recv()
            padded = jnp.concatenate(
                [st_recv[slot, chunk], jnp.zeros((120, rows), jnp.float32)], axis=0
            )
            levels_in.append(jnp.transpose(padded))
        for inner in range(BUNDLE):
            where = head_cols(chunk * BUNDLE + inner)
            blended, peak, total = attend(q_ref[:, where], pieces_of(chunk * BUNDLE + inner))
            if slots:
                levels = [peak + jnp.log2(total)]
                outs = [blended]
                for slot, level in zip(slots, levels_in):
                    levels.append(level[:, inner : inner + 1])
                    outs.append(o_recv[slot, :, where].astype(jnp.float32))
                top = functools.reduce(jnp.maximum, levels)
                shares = [jnp.exp2(level - top) for level in levels]
                whole = functools.reduce(jnp.add, shares)
                blended = functools.reduce(
                    jnp.add, [out * share for out, share in zip(outs, shares)]
                ) / whole
            out_ref[:, where] = blended.astype(jnp.bfloat16)

    def loop(low, high, body):
        def step(chunk, carry):
            body(chunk)
            return carry
        lax.fori_loop(low, high, step, 0)

    def pair(ref, head, low=None, high=None):
        part = slice(low, high)
        return ref[part, head_cols(head)], ref[part, head_cols(head, WIDTH)]

    def prompt_copy(kind, piece, line, index, to_line, own=False):
        return remote(
            prompt_ref if own else bank.at[piece, line], bank.at[piece, line],
            pr_s.at[kind, piece], pr_r.at[kind if kind > 1 else 0, piece], index, to_line,
        )

    def line_copies(here, piece):
        own = here == piece
        copies = []
        if piece <= here < WIN - 1:
            copies.append(prompt_copy(0, piece, stream, here + 1, stream, own))
        if 0 < here <= piece:
            copies.append(prompt_copy(1, piece, stream, here - 1, stream, own))
        copies.append(prompt_copy(2, piece, stream, here, across, own))
        copies.append(prompt_copy(3, piece, stream, here, beside, own))
        return copies

    def own_copy(here):
        return pltpu.make_async_copy(prompt_ref, bank.at[here, stream], own_sem)

    def spread(here, piece):
        if not with_prompts:
            return
        if piece != here:
            prompt_copy(0, piece, stream, here, stream).wait_recv()
        for copy in line_copies(here, piece):
            copy.start()

    def spread_across(here, pieces):
        if not with_prompts:
            return
        for piece in pieces:
            prompt_copy(2, piece, across, here, stream).wait_recv()
            prompt_copy(4, piece, across, here, beside).start()

    def cross(here):
        if not with_prompts:
            return
        own_copy(here).wait()
        for piece in range(WIN):
            prompt_copy(3, piece, beside, here, stream).wait_recv()
            prompt_copy(4, piece, 3 - stream, here, stream).wait_recv()
        pick = pick_ref[0]
        tokens = bank.shape[0] * bank.shape[1] * bank.shape[3]

        def chunk_of(chunk):
            for inner in range(BUNDLE):
                head = chunk * BUNDLE + inner
                keys = bank[:, :, pick, :, head_cols(head)].reshape(tokens, HDIM)
                values = bank[:, :, pick, :, head_cols(head, WIDTH)].reshape(tokens, HDIM)
                blended, _, _ = attend(cq_ref[:, head_cols(head)], [(keys, values)])
                cross_ref[:, head_cols(head)] = blended.astype(jnp.bfloat16)
        loop(0, CHUNKS, chunk_of)

    def drain_prompts(here):
        if not with_prompts:
            return
        for piece in range(WIN):
            for copy in line_copies(here, piece):
                copy.wait_send()
            prompt_copy(4, piece, across, here, beside).wait_send()

    barrier = pltpu.get_barrier_semaphore()
    greeted = [at_place((place + step) % WIN) for step in range(1, WIN)]
    if with_prompts:
        greeted += [{"span": place * stride + across}, {"span": place * stride + beside}]
    for other in greeted:
        pl.semaphore_signal(barrier, inc=1, device_id=other, device_id_type=MESH)
    pl.semaphore_wait(barrier, len(greeted))

    @pl.when(place == 0)
    def _():
        spread(0, 0)

        def send(chunk):
            for copy in kv_copies(chunk):
                copy.start()
        loop(0, CHUNKS, send)
        if with_prompts:
            own_copy(0).start()
        sinks[0:rows_s, :] = sink_ref[...]
        spread(0, 1)
        spread(0, 2)
        spread(0, 3)
        spread_across(0, range(WIN))
        cross(0)
        for which in (1, 2, 3):
            sink_copy(which, 0, False).wait_recv()
        loop(0, CHUNKS, lambda chunk: final(
            chunk, lambda head: [pair(sinks, head), pair(kv_ref, head)], (), 0
        ))

        def drain(chunk):
            for copy in kv_copies(chunk):
                copy.wait_send()
        loop(0, CHUNKS, drain)
        drain_prompts(0)

    @pl.when(place == 1)
    def _():
        spread(1, 1)
        sink_copy(1, 0, True).start()
        if with_prompts:
            own_copy(1).start()
        sinks[rows_s : 2 * rows_s, :] = sink_ref[...]

        def work(chunk):
            for copy in kv_copies(chunk):
                copy.wait_recv()
            for slot in range(2):
                q_copy(chunk, slot, 1).wait_recv()
                partial(
                    slot, chunk,
                    lambda head: [
                        pair(sinks, head, 0, 2 * rows_s), pair(kv_prev, head), pair(kv_ref, head)
                    ],
                    2 + slot,
                )

        def ending(chunk):
            final(
                chunk, lambda head: [pair(sinks, head), pair(kv_prev, head), pair(kv_ref, head)], (), 1
            )
        spread(1, 0)
        spread(1, 2)
        loop(0, 1, work)
        spread(1, 3)
        loop(1, 2, work)
        sink_copy(3, 1, False).wait_recv()
        sink_copy(3, 0, False).start()
        loop(2, 3, work)
        sink_copy(2, 1, False).wait_recv()
        sink_copy(2, 0, False).start()
        spread_across(1, range(WIN))
        loop(3, CHUNKS - 1, work)
        cross(1)
        loop(0, CHUNKS - 1, ending)
        loop(CHUNKS - 1, CHUNKS, work)
        loop(CHUNKS - 1, CHUNKS, ending)
        for which in (1, 2, 3):
            sink_copy(which, 0, which == 1).wait_send()
        for slot in range(2):
            drain_partial(slot, 2 + slot)
        drain_prompts(1)

    @pl.when(place == 2)
    def _():
        spread(2, 2)
        q_copy(0, 0, 1).start()
        if with_prompts:
            own_copy(2).start()
        sinks[2 * rows_s : 3 * rows_s, :] = sink_ref[...]
        spread(2, 1)
        spread(2, 3)
        q_copy(1, 0, 1).start()
        spread(2, 0)
        sink_copy(3, 2, False).wait_recv()
        sink_copy(3, 1, False).start()
        q_copy(2, 0, 1).start()
        sink_copy(2, 1, True).start()
        loop(3, CHUNKS, lambda chunk: q_copy(chunk, 0, 1).start())
        spread_across(2, range(WIN))

        def work(chunk):
            q_copy(chunk, 0, 2).wait_recv()
            partial(
                0, chunk,
                lambda head: [pair(sinks, head, 2 * rows_s, 3 * rows_s), pair(kv_ref, head)], 3,
            )
        cross(2)
        loop(0, CHUNKS, work)
        loop(0, CHUNKS, lambda chunk: final(
            chunk, lambda head: [pair(sinks, head, 2 * rows_s, 4 * rows_s), pair(kv_ref, head)], (0,), 2
        ))
        sink_copy(2, 1, True).wait_send()
        sink_copy(3, 1, False).wait_send()
        loop(0, CHUNKS, lambda chunk: q_copy(chunk, 0, 1).wait_send())
        drain_partial(0, 3)
        drain_prompts(2)

    @pl.when(place == 3)
    def _():
        spread(3, 3)
        sink_copy(3, 2, True).start()
        loop(0, CHUNKS, lambda chunk: q_copy(chunk, 1, 1).start())
        loop(0, CHUNKS, lambda chunk: q_copy(chunk, 0, 2).start())
        if with_prompts:
            own_copy(3).start()
        spread(3, 2)
        spread(3, 1)
        spread(3, 0)
        spread_across(3, range(WIN - 1, -1, -1))
        cross(3)
        loop(0, CHUNKS, lambda chunk: final(
            chunk, lambda head: [pair(sink_ref, head), pair(kv_ref, head)], (0, 1), 3
        ))
        sink_copy(3, 2, True).wait_send()
        loop(0, CHUNKS, lambda chunk: q_copy(chunk, 1, 1).wait_send())
        loop(0, CHUNKS, lambda chunk: q_copy(chunk, 0, 2).wait_send())
        drain_prompts(3)


def self_attention(queries, frame_kv, own_sink, prompts=None):
    rows = queries.shape[0]
    vmem = pl.BlockSpec(memory_space=pltpu.VMEM)
    dma = pltpu.SemaphoreType.DMA
    operands = [queries, frame_kv, own_sink]
    in_specs = [vmem] * 3
    outs = [jax.ShapeDtypeStruct((rows, WIDTH), jnp.bfloat16)]
    scratch = []
    if prompts is not None:
        operands += prompts
        in_specs += [vmem, vmem, pl.BlockSpec(memory_space=pltpu.SMEM)]
        outs = outs * 2
        scratch = [
            pltpu.VMEM((WIN, lax.axis_size("span") // WIN) + prompts[0].shape, jnp.bfloat16),
            dma((5, WIN)), dma((5, WIN)), dma,
        ]
    return pl.pallas_call(
        functools.partial(self_kernel, prompts is not None),
        out_shape=outs,
        in_specs=in_specs,
        out_specs=[vmem] * len(outs),
        scratch_shapes=scratch + [
            pltpu.VMEM((rows, 2 * WIDTH), jnp.bfloat16),
            pltpu.VMEM((WIN * own_sink.shape[0], 2 * WIDTH), jnp.bfloat16),
            pltpu.VMEM((2, rows, WIDTH), jnp.bfloat16),
            pltpu.VMEM((2, rows, WIDTH), jnp.bfloat16),
            pltpu.VMEM((2, rows, WIDTH), jnp.bfloat16),
            pltpu.VMEM((2, CHUNKS, 8, rows), jnp.float32),
            pltpu.VMEM((2, CHUNKS, 8, rows), jnp.float32),
            dma((4, CHUNKS)), dma((4, CHUNKS)),
            dma((2, CHUNKS)), dma((2, CHUNKS)),
            dma((WIN,)), dma((WIN,)),
            dma((2, CHUNKS)), dma((2, CHUNKS)),
            dma((2, CHUNKS)), dma((2, CHUNKS)),
        ],
        compiler_params=pltpu.CompilerParams(
            collective_id=0, has_side_effects=True, vmem_limit_bytes=60 * 1024 * 1024
        ),
    )(*operands)


def cross_kernel(pick_ref, q_ref, k_ref, v_ref, out_ref):
    for inner in range(BUNDLE):
        where = slice(inner * HDIM, (inner + 1) * HDIM)
        blended, _, _ = attend(q_ref[:, where], [(k_ref[0, :, where], v_ref[0, :, where])])
        out_ref[:, where] = blended.astype(jnp.bfloat16)


def cross_attention(cross_queries, prompts, pick):
    rows = cross_queries.shape[0]
    tokens = prompts.shape[1]
    return pl.pallas_call(
        cross_kernel,
        out_shape=jax.ShapeDtypeStruct((rows, WIDTH), jnp.bfloat16),
        grid_spec=pltpu.PrefetchScalarGridSpec(
            num_scalar_prefetch=1,
            grid=(CHUNKS,),
            in_specs=[
                pl.BlockSpec((rows, BW), lambda c, pick: (0, c)),
                pl.BlockSpec((1, tokens, BW), lambda c, pick: (pick[0], 0, c)),
                pl.BlockSpec((1, tokens, BW), lambda c, pick: (pick[0], 0, CHUNKS + c)),
            ],
            out_specs=pl.BlockSpec((rows, BW), lambda c, pick: (0, c)),
        ),
    )(pick.reshape(1), cross_queries, prompts, prompts)


def shards(queries, cross_queries, frame_kv, sink_kv, prompt_kv, switch):
    stream_count = lax.axis_size("span") // WIN
    device = lax.axis_index("span")
    place = device // stream_count
    stream_of = device % stream_count
    stream_ids = jnp.arange(switch.shape[0], dtype=jnp.int32)
    switch_at = jnp.sum(jnp.where(stream_ids == stream_of, switch, 0))
    pick = (place >= switch_at).astype(jnp.int32)
    own_sink = sink_kv.reshape(sink_kv.shape[1], sink_kv.shape[2])
    if stream_count == 4 and prompt_kv.shape[1] % 16 == 0:
        return tuple(
            self_attention(queries, frame_kv, own_sink, [prompt_kv, cross_queries, pick.reshape(1)])
        )
    prompts = lax.all_gather(prompt_kv, "span", axis=1, tiled=True)
    (self_out,) = self_attention(queries, frame_kv, own_sink)
    cross_out = cross_attention(cross_queries, prompts, pick)
    return (self_out, cross_out)


def solution(mesh):
    in_specs = (
        P(("groups", "span"), None),
        P(("groups", "span"), None),
        P(("groups", "span"), None),
        P(("groups", "span"), None, None),
        P("groups", "span", None),
        P("groups"),
    )
    out_specs = (P(("groups", "span"), None), P(("groups", "span"), None))
    return jax.shard_map(shards, mesh=mesh, in_specs=in_specs, out_specs=out_specs, check_vma=False)
```

time: 209 us -> 156 us (0.75)
  Pallas kernels: 191 us -> 149 us
  between operations: 14.7 us -> 1.32 us
  local copies, waits for them, and re-layouts: 1.06 us -> 3.62 us
    pallas_call x2 -> x1, Pallas kernels: 191 us -> 149 us  [self_attention(): pl.pallas_call(functools.partial(self_kernel, prompts is not None), out_s...]
    unnamed x3 -> x4, local copies, waits for them, and re-layouts: 1.06 us -> 3.62 us
  transfers between devices with their start and end apart: 1 -> 0, of which waited for: 0 -> 0; matrix products, arithmetic and copies ran while one was open for 1% -> 0% of each run, Pallas kernels for 87% -> 0%
where the time goes in v2:
time: 156 us
  Pallas kernels  149 us (96%)
  local copies, waits for them, and re-layouts  3.62 us (2%)
    pallas_call x1, Pallas kernels, self_attention(): pl.pallas_call(functools.partial(self_kernel, prompts is not None), out_s...  149 us
    unnamed x4, local copies, waits for them, and re-layouts  3.62 us

profile of v2, /device:TPU:24, one launch (start us, length us, event | category | flops | bytes accessed | tf_op | source)
XLA Modules:
  0.0 155.6 jit_solution(3047201459728542700)
XLA Ops:
  0.7 1.3 fusion
  2.6 149.4 %shard_map.77 = (bf16[256,2560]{1,0:T(8,128)(2,1)}, bf16[256,2560]{1,0:T(8,128)(2,1)}) custom-call(bf16[256,2560]{1,0:T(8,128)(2,1)} %refs_0_.1, bf16[256,5120]{1,0:T(8,128)(2,1)} %refs_1_.1, bf16[64,5120]{1,0:T(8,128)(2,1)} %bitcast.2, bf16[2,32,5120]{2,1,0:T(8,128)(2,1)} %refs_3_.1, bf16[256,2560]{1,0:T(8,128)(2,1)} %refs_4_.1, s32[1]{0:T(128)} %bitcast.1.refs_5_), custom_call_target="tpu_custom_call" | custom-call | tf_op jit(solution)/shard_map/pallas_call | solution.py:385
  152.0 0.0 copy-start
  152.0 2.6 %copy.10 = bf16[256,2560]{1,0:T(8,128)(2,1)} copy(bf16[256,2560]{1,0:T(8,128)(2,1)} %get-tuple-element.4) | data formatting | bytes 2621440
  154.6 0.0 copy-done
  154.6 1.1 copy.11
Async XLA Ops:
  152.0 2.6 %copy-start = (bf16[256,2560]{1,0:T(8,128)(2,1)S(1)}, bf16[256,2560]{1,0:T(8,128)(2,1)}, u32[]{:S(2)}) copy-start(bf16[256,2560]{1,0:T(8,128)(2,1)} %get-tuple-element.5) | copy-start | bytes 3932164

commit v3 on v2

--- a/solution.py
+++ b/solution.py
@@ -90,6 +90,12 @@
         return remote(
             q_ref.at[:, cols(chunk)], q_in.at[slot, :, cols(chunk)],
             q_s.at[slot, chunk], q_r.at[slot, chunk], index,
+        )
+
+    def q_relay(chunk):
+        return remote(
+            q_in.at[0, :, cols(chunk)], q_in.at[1, :, cols(chunk)],
+            q_s.at[1, chunk], q_r.at[1, chunk], 1,
         )
 
     def sink_copy(which, index, own):
@@ -206,7 +212,7 @@
         for piece in range(WIN):
             prompt_copy(3, piece, beside, here, stream).wait_recv()
             prompt_copy(4, piece, 3 - stream, here, stream).wait_recv()
-        pick = pick_ref[0]
+        pick = (place >= pick_ref[stream]).astype(jnp.int32)
         tokens = bank.shape[0] * bank.shape[1] * bank.shape[3]
 
         def chunk_of(chunk):
@@ -289,20 +295,20 @@
             )
         spread(1, 0)
         spread(1, 2)
-        loop(0, 1, work)
         spread(1, 3)
-        loop(1, 2, work)
+        loop(0, 2, work)
         sink_copy(3, 1, False).wait_recv()
         sink_copy(3, 0, False).start()
-        loop(2, 3, work)
+        spread_across(1, range(WIN))
         sink_copy(2, 1, False).wait_recv()
         sink_copy(2, 0, False).start()
-        spread_across(1, range(WIN))
-        loop(3, CHUNKS - 1, work)
         cross(1)
-        loop(0, CHUNKS - 1, ending)
-        loop(CHUNKS - 1, CHUNKS, work)
-        loop(CHUNKS - 1, CHUNKS, ending)
+        loop(0, 2, ending)
+
+        def both(chunk):
+            work(chunk)
+            ending(chunk)
+        loop(2, CHUNKS, both)
         for which in (1, 2, 3):
             sink_copy(which, 0, which == 1).wait_send()
         for slot in range(2):
@@ -316,19 +322,27 @@
         if with_prompts:
             own_copy(2).start()
         sinks[2 * rows_s : 3 * rows_s, :] = sink_ref[...]
+        spread(2, 3)
         spread(2, 1)
-        spread(2, 3)
+
+        def relay(chunk):
+            q_copy(chunk, 0, 2).wait_recv()
+            q_relay(chunk).start()
+        relay(0)
         q_copy(1, 0, 1).start()
+        relay(1)
         spread(2, 0)
         sink_copy(3, 2, False).wait_recv()
         sink_copy(3, 1, False).start()
-        q_copy(2, 0, 1).start()
         sink_copy(2, 1, True).start()
-        loop(3, CHUNKS, lambda chunk: q_copy(chunk, 0, 1).start())
+
+        def send(chunk):
+            q_copy(chunk, 0, 1).start()
+            relay(chunk)
+        loop(2, CHUNKS, send)
         spread_across(2, range(WIN))
 
         def work(chunk):
-            q_copy(chunk, 0, 2).wait_recv()
             partial(
                 0, chunk,
                 lambda head: [pair(sinks, head, 2 * rows_s, 3 * rows_s), pair(kv_ref, head)], 3,
@@ -341,15 +355,16 @@
         sink_copy(2, 1, True).wait_send()
         sink_copy(3, 1, False).wait_send()
         loop(0, CHUNKS, lambda chunk: q_copy(chunk, 0, 1).wait_send())
+        loop(0, CHUNKS, lambda chunk: q_relay(chunk).wait_send())
         drain_partial(0, 3)
         drain_prompts(2)
 
     @pl.when(place == 3)
     def _():
         spread(3, 3)
+        loop(0, 2, lambda chunk: q_copy(chunk, 0, 2).start())
         sink_copy(3, 2, True).start()
-        loop(0, CHUNKS, lambda chunk: q_copy(chunk, 1, 1).start())
-        loop(0, CHUNKS, lambda chunk: q_copy(chunk, 0, 2).start())
+        loop(2, CHUNKS, lambda chunk: q_copy(chunk, 0, 2).start())
         if with_prompts:
             own_copy(3).start()
         spread(3, 2)
@@ -361,7 +376,6 @@
             chunk, lambda head: [pair(sink_ref, head), pair(kv_ref, head)], (0, 1), 3
         ))
         sink_copy(3, 2, True).wait_send()
-        loop(0, CHUNKS, lambda chunk: q_copy(chunk, 1, 1).wait_send())
         loop(0, CHUNKS, lambda chunk: q_copy(chunk, 0, 2).wait_send())
         drain_prompts(3)
 
@@ -438,14 +452,14 @@
     device = lax.axis_index("span")
     place = device // stream_count
     stream_of = device % stream_count
+    own_sink = sink_kv.reshape(sink_kv.shape[1], sink_kv.shape[2])
+    if stream_count == 4 and prompt_kv.shape[1] % 16 == 0:
+        return tuple(
+            self_attention(queries, frame_kv, own_sink, [prompt_kv, cross_queries, switch])
+        )
     stream_ids = jnp.arange(switch.shape[0], dtype=jnp.int32)
     switch_at = jnp.sum(jnp.where(stream_ids == stream_of, switch, 0))
     pick = (place >= switch_at).astype(jnp.int32)
-    own_sink = sink_kv.reshape(sink_kv.shape[1], sink_kv.shape[2])
-    if stream_count == 4 and prompt_kv.shape[1] % 16 == 0:
-        return tuple(
-            self_attention(queries, frame_kv, own_sink, [prompt_kv, cross_queries, pick.reshape(1)])
-        )
     prompts = lax.all_gather(prompt_kv, "span", axis=1, tiled=True)
     (self_out,) = self_attention(queries, frame_kv, own_sink)
     cross_out = cross_attention(cross_queries, prompts, pick)

time: 156 us -> 142 us (0.910)
  Pallas kernels: 149 us -> 137 us
    pallas_call x1, Pallas kernels: 149 us -> 137 us  [self_attention(): pl.pallas_call(functools.partial(self_kernel, prompts is not None), out_s...]
where the time goes in v3:
time: 142 us; the launch traced here: 141 us
  Pallas kernels  137 us (96%)
  local copies, waits for them, and re-layouts  3.62 us (3%)
    pallas_call x1, Pallas kernels, self_attention(): pl.pallas_call(functools.partial(self_kernel, prompts is not None), out_s...  137 us
    unnamed x4, local copies, waits for them, and re-layouts  3.62 us

profile of v3, /device:TPU:24, one launch (start us, length us, event | category | flops | bytes accessed | tf_op | source)
XLA Modules:
  0.0 141.4 jit_solution(5458880600434110739)
XLA Ops:
  0.6 137.1 %shard_map.77 = (bf16[256,2560]{1,0:T(8,128)(2,1)}, bf16[256,2560]{1,0:T(8,128)(2,1)}) custom-call(bf16[256,2560]{1,0:T(8,128)(2,1)} %refs_0_.1, bf16[256,5120]{1,0:T(8,128)(2,1)} %refs_1_.1, bf16[64,5120]{1,0:T(8,128)(2,1)} %bitcast.1, bf16[2,32,5120]{2,1,0:T(8,128)(2,1)} %refs_3_.1, bf16[256,2560]{1,0:T(8,128)(2,1)} %refs_4_.1, s32[4]{0:T(128)} %refs_5_.1), custom_call_target="tpu_custom_call" | custom-call | tf_op jit(solution)/shard_map/pallas_call | solution.py:399
  137.8 0.0 copy-start
  137.8 2.6 %copy.10 = bf16[256,2560]{1,0:T(8,128)(2,1)} copy(bf16[256,2560]{1,0:T(8,128)(2,1)} %get-tuple-element.4) | data formatting | bytes 2621440
  140.3 0.0 copy-done
  140.3 1.1 copy.11
Async XLA Ops:
  137.8 2.6 %copy-start = (bf16[256,2560]{1,0:T(8,128)(2,1)S(1)}, bf16[256,2560]{1,0:T(8,128)(2,1)}, u32[]{:S(2)}) copy-start(bf16[256,2560]{1,0:T(8,128)(2,1)} %get-tuple-element.5) | copy-start | bytes 3932164
